TPU v7x, 32 devices: a whole 2x2x4 slice. The times are simulated.
32 devices in a mesh: space: 8 (over z, y), view: 4 (over x, core).
Axes of the slice: x: 2, y: 2, z: 4, core: 2. Of those that a mesh axis runs over, the one named last changes fastest.
Arguments:
- params: float32 [59, 16384], P(None, 'space'), may hold values from -8 to 514, as said below
- visible: int32 [8, 128, 16], P('space'), may hold values from 0 to 2047, as said below
- blocks: int32 [8, 128], P('space'), may hold values from 0 to 63, as said below
- counts: int32 [8, 8], P('space'), may hold values from 1 to 16
- depth_rank: int32 [4, 8], P('view'), may hold values from 0 to 7, each once within a row
- camera: float32 [4, 3], P('view'), may hold values from -0.006 to 0.006
- background: float32 [4, 3], P('view'), may hold values from 0 to 1
- target: float32 [4, 3, 128, 512], P('view', None, 'space'), may hold values from 0 to 1
Outputs:
- grad_params: float32 [59, 16384], P(None, 'space')
- rendered: float32 [4, 3, 128, 512], P('view', None, 'space')
- loss: float32 [4], P('view')
Inputs may be any that keep to these rules, and one draw needn't show every extreme that they name: `visible`: each row of a subspace's table lists 16 different splats of that subspace in increasing order; every splat of the subspace is listed exactly once. Slot j of a subspace goes to owner j // 16; the 16 slots that one subspace sends to one owner name different blocks. counts[s, o] live slots lead the 16 slots that subspace s sends to owner o. `params`: rows 6 to 9 of a column hold a quaternion whose first component lies in [1, 2].
All inputs are finite; a program needn't handle non-finite values.
Results may differ from a plain program's by a relative error of at most 0.0003.
Values sent between devices are 32-bit elements; how exact they have to be, the bound alone decides.
A program may use at most 64 MiB of HBM per device.

v0:
```python
import math
import jax
import jax.numpy as jnp
from jax import lax
from jax.sharding import PartitionSpec as P

HIGHEST = lax.Precision.HIGHEST
SH_ZERO = 0.28209479177387814
SH_ONE = 0.4886025119029199
SH_TWO = (
    1.0925484305920792,
    -1.0925484305920792,
    0.31539156525252005,
    -1.0925484305920792,
    0.5462742152960396,
)
SH_THREE = (
    -0.5900435899266435,
    2.890611442640554,
    -0.4570457994644658,
    0.3731763325901154,
    -0.4570457994644658,
    1.445305721320277,
    -0.5900435899266435,
)
DILATION = 0.3
SMOOTHING = 0.0001
SSIM_FIRST = 0.0001
SSIM_SECOND = 0.0009


def with_halo(x, sides, width):
    for axis, dim in sides:
        devices, length = (lax.axis_size(axis), x.shape[dim])
        up = [(i, (i + 1) % devices) for i in range(devices - 1)]
        down = [(j, i) for i, j in up]
        last = lax.slice_in_dim(x, length - width, length, axis=dim)
        first = lax.slice_in_dim(x, 0, width, axis=dim)
        before = lax.ppermute(last, axis, up)
        after = lax.ppermute(first, axis, down)
        x = jnp.concatenate([before, x, after], axis=dim)
    return x


def passed_along(x, axis, by):
    devices = lax.axis_size(axis)
    pairs = [(i, i + by) for i in range(devices) if 0 <= i + by < devices]
    return lax.ppermute(x, axis, pairs)


def camera_rotation(angles):
    cos_a, sin_a = (jnp.cos(angles[0]), jnp.sin(angles[0]))
    cos_b, sin_b = (jnp.cos(angles[1]), jnp.sin(angles[1]))
    cos_c, sin_c = (jnp.cos(angles[2]), jnp.sin(angles[2]))
    unity = jnp.ones_like(cos_a)
    nought = jnp.zeros_like(cos_a)
    turn_x = jnp.stack(
        [
            jnp.stack([unity, nought, nought]),
            jnp.stack([nought, cos_a, -sin_a]),
            jnp.stack([nought, sin_a, cos_a]),
        ]
    )
    turn_y = jnp.stack(
        [
            jnp.stack([cos_b, nought, sin_b]),
            jnp.stack([nought, unity, nought]),
            jnp.stack([-sin_b, nought, cos_b]),
        ]
    )
    turn_z = jnp.stack(
        [
            jnp.stack([cos_c, -sin_c, nought]),
            jnp.stack([sin_c, cos_c, nought]),
            jnp.stack([nought, nought, unity]),
        ]
    )
    return jnp.dot(jnp.dot(turn_z, turn_y, precision=HIGHEST), turn_x, precision=HIGHEST)


def harmonics(view_axis):
    axis_x, axis_y, axis_z = (view_axis[0], view_axis[1], view_axis[2])
    sq_x, sq_y, sq_z = (axis_x * axis_x, axis_y * axis_y, axis_z * axis_z)
    values = [
        SH_ZERO * jnp.ones_like(axis_x),
        -SH_ONE * axis_y,
        SH_ONE * axis_z,
        -SH_ONE * axis_x,
        SH_TWO[0] * axis_x * axis_y,
        SH_TWO[1] * axis_y * axis_z,
        SH_TWO[2] * (2.0 * sq_z - sq_x - sq_y),
        SH_TWO[3] * axis_x * axis_z,
        SH_TWO[4] * (sq_x - sq_y),
        SH_THREE[0] * axis_y * (3.0 * sq_x - sq_y),
        SH_THREE[1] * axis_x * axis_y * axis_z,
        SH_THREE[2] * axis_y * (4.0 * sq_z - sq_x - sq_y),
        SH_THREE[3] * axis_z * (2.0 * sq_z - 3.0 * sq_x - 3.0 * sq_y),
        SH_THREE[4] * axis_x * (4.0 * sq_z - sq_x - sq_y),
        SH_THREE[5] * axis_z * (sq_x - sq_y),
        SH_THREE[6] * axis_x * (sq_x - 3.0 * sq_y),
    ]
    return jnp.stack(values)


def project(param_in, angles, centre_x, centre_y):
    turn = camera_rotation(angles)
    scales = jnp.exp(param_in[3:6])
    quaternion = param_in[6:10]
    quaternion = quaternion / jnp.sqrt(jnp.sum(quaternion * quaternion, axis=0))
    part_w, part_x, part_y, part_z = (quaternion[0], quaternion[1], quaternion[2], quaternion[3])
    spin = [
        [
            1.0 - 2.0 * (part_y * part_y + part_z * part_z),
            2.0 * (part_x * part_y - part_w * part_z),
            2.0 * (part_x * part_z + part_w * part_y),
        ],
        [
            2.0 * (part_x * part_y + part_w * part_z),
            1.0 - 2.0 * (part_x * part_x + part_z * part_z),
            2.0 * (part_y * part_z - part_w * part_x),
        ],
        [
            2.0 * (part_x * part_z - part_w * part_y),
            2.0 * (part_y * part_z + part_w * part_x),
            1.0 - 2.0 * (part_x * part_x + part_y * part_y),
        ],
    ]
    frame = [
        [
            (
                turn[row, 0] * spin[0][col]
                + turn[row, 1] * spin[1][col]
                + turn[row, 2] * spin[2][col]
            )
            * scales[col]
            for col in range(3)
        ]
        for row in range(2)
    ]
    cov_xx = (
        frame[0][0] * frame[0][0] + frame[0][1] * frame[0][1] + frame[0][2] * frame[0][2] + DILATION
    )
    cov_xy = frame[0][0] * frame[1][0] + frame[0][1] * frame[1][1] + frame[0][2] * frame[1][2]
    cov_yy = (
        frame[1][0] * frame[1][0] + frame[1][1] * frame[1][1] + frame[1][2] * frame[1][2] + DILATION
    )
    determinant = cov_xx * cov_yy - cov_xy * cov_xy
    shift_x = param_in[0] - centre_x
    shift_y = param_in[1] - centre_y
    mean_u = turn[0, 0] * shift_x + turn[0, 1] * shift_y + turn[0, 2] * param_in[2] + centre_x
    mean_w = turn[1, 0] * shift_x + turn[1, 1] * shift_y + turn[1, 2] * param_in[2] + centre_y
    opacity = jax.nn.sigmoid(param_in[10])
    basis = harmonics(turn[2])
    coeffs = param_in[11:59].reshape(16, 3, param_in.shape[1])
    colour = 0.5 + jnp.sum(basis[:, None, None] * coeffs, axis=0)
    record = jnp.stack(
        [mean_u, mean_w, cov_yy / determinant, -cov_xy / determinant, cov_xx / determinant, opacity]
    )
    return jnp.concatenate([record, colour], axis=0)


def make_projector(view_angles, centre_x, centre_y):

    def apply(param_in):
        return project(param_in, view_angles, centre_x, centre_y)

    return apply


def render(gathered, grid_x, grid_y):
    delta_x = grid_x[:, None, :] - gathered[0][:, :, None]
    delta_y = grid_y[:, None, :] - gathered[1][:, :, None]
    powers = 0.5 * (
        gathered[2][:, :, None] * delta_x * delta_x
        + 2.0 * gathered[3][:, :, None] * delta_x * delta_y
        + gathered[4][:, :, None] * delta_y * delta_y
    )
    alphas = gathered[5][:, :, None] * jnp.exp(-powers)
    kept_log = jnp.log1p(-alphas)
    before = jnp.cumsum(kept_log, axis=1) - kept_log
    weights = alphas * jnp.exp(before)
    colour = jnp.einsum("skp,csk->scp", weights, gathered[6:9], precision=HIGHEST)
    return jnp.concatenate([colour, jnp.sum(kept_log, axis=1)[:, None, :]], axis=1)


def pixel_grid(owners, blocks_used, strip_rows, block_cols):
    inner = jnp.arange(128, dtype=jnp.int32)
    corner_y = owners * strip_rows + blocks_used // block_cols * 8
    corner_x = blocks_used % block_cols * 16
    grid_y = (corner_y[:, None] + inner[None, :] // 16).astype(jnp.float32) + 0.5
    grid_x = (corner_x[:, None] + inner[None, :] % 16).astype(jnp.float32) + 0.5
    return (grid_x, grid_y)


def composite(pieces, target_ids, depth_ranks, backdrop, block_rows, block_cols):
    block_count = block_rows * block_cols
    onehot = (
        target_ids[:, :, None] == jnp.arange(block_count, dtype=jnp.int32)[None, None, :]
    ).astype(jnp.float32)
    dense = jnp.einsum("scb,scqp->bsqp", onehot, pieces, precision=HIGHEST)
    kept_log = dense[:, :, 3]
    nearer = (depth_ranks[None, :] < depth_ranks[:, None]).astype(jnp.float32)
    before = jnp.einsum("st,btp->bsp", nearer, kept_log, precision=HIGHEST)
    picture = jnp.einsum("bsp,bscp->bcp", jnp.exp(before), dense[:, :, 0:3], precision=HIGHEST)
    picture = picture + backdrop[None, :, None] * jnp.exp(jnp.sum(kept_log, axis=1))[:, None, :]
    picture = picture.reshape(block_rows, block_cols, 3, 8, 16).transpose(2, 0, 3, 1, 4)
    return picture.reshape(3, block_rows * 8, block_cols * 16)


def blur_taps():
    raw_taps = [math.exp(-(offset - 5) * (offset - 5) / 4.5) for offset in range(11)]
    total = sum(raw_taps)
    return [value / total for value in raw_taps]


def blur(values, count):
    taps = blur_taps()
    width_px = values.shape[2]
    padded = jnp.pad(values, ((0, 0), (0, 0), (5, 5)))
    across = taps[0] * padded[:, :, 0:width_px]
    for offset in range(1, 11):
        across = across + taps[offset] * padded[:, :, offset : offset + width_px]
    result = taps[0] * across[:, 0:count]
    for offset in range(1, 11):
        result = result + taps[offset] * across[:, offset : offset + count]
    return result


def pixel_terms(picture, goal, count):
    mean_a = blur(picture, count)
    mean_b = blur(goal, count)
    var_a = blur(picture * picture, count) - mean_a * mean_a
    var_b = blur(goal * goal, count) - mean_b * mean_b
    cov_ab = blur(picture * goal, count) - mean_a * mean_b
    ssim = (
        (2.0 * mean_a * mean_b + SSIM_FIRST)
        * (2.0 * cov_ab + SSIM_SECOND)
        / ((mean_a * mean_a + mean_b * mean_b + SSIM_FIRST) * (var_a + var_b + SSIM_SECOND))
    )
    differ = picture[:, 5 : 5 + count] - goal[:, 5 : 5 + count]
    return 0.8 * jnp.sqrt(differ * differ + SMOOTHING) + 0.2 * (1.0 - ssim)


def shards(params, visible, blocks, counts, depth_rank, camera, background, target):
    devices = lax.axis_size("space")
    me_index = lax.axis_index("space")
    slot_total = visible.shape[1]
    list_length = visible.shape[2]
    capacity = slot_total // devices
    strip_rows = target.shape[2]
    width_px = target.shape[3]
    block_rows = strip_rows // 8
    block_cols = width_px // 16
    height_px = strip_rows * devices
    lists = visible[0]
    slot_blocks = blocks[0]
    live = jnp.arange(capacity, dtype=jnp.int32)[None, :] < counts[0][:, None]
    target_ids = jnp.where(live, slot_blocks.reshape(devices, capacity), -1)
    centre_x = 0.5 * width_px
    centre_y = 0.5 * height_px
    records, pull_project = jax.vjp(make_projector(camera[0], centre_x, centre_y), params)

    def sender_side(record_in):
        picked = record_in[:, lists]
        return picked.reshape(9, devices, capacity * list_length).transpose(1, 0, 2)

    message, pull_sender = jax.vjp(sender_side, records)
    received, recv_ids = (
        lax.all_to_all(message, "space", split_axis=0, concat_axis=0, tiled=True),
        lax.all_to_all(target_ids, "space", split_axis=0, concat_axis=0, tiled=True),
    )
    own_blocks = jnp.maximum(recv_ids.reshape(devices * capacity), 0)
    grid_x, grid_y = pixel_grid(
        jnp.full(own_blocks.shape, me_index, jnp.int32), own_blocks, strip_rows, block_cols
    )

    def owner_side(recv_in):
        gathered = (
            recv_in.reshape(devices, 9, capacity, list_length)
            .transpose(1, 0, 2, 3)
            .reshape(9, devices * capacity, list_length)
        )
        pieces = render(gathered, grid_x, grid_y).reshape(devices, capacity, 4, 128)
        return composite(pieces, recv_ids, depth_rank[0], background[0], block_rows, block_cols)

    strip, pull_owner = jax.vjp(owner_side, received)
    stacked = jnp.concatenate([strip, target[0]], axis=0)
    extended = with_halo(stacked, (("space", 1),), 5)
    goal = extended[3:6]

    def local_sum(picture):
        return jnp.sum(pixel_terms(picture, goal, strip_rows))

    own_loss, pull_terms = jax.vjp(local_sum, extended[0:3])
    grad_extended = pull_terms(jnp.ones((), jnp.float32))[0]
    from_below = passed_along(grad_extended[:, 0:5], "space", -1)
    from_above = passed_along(grad_extended[:, strip_rows + 5 : strip_rows + 10], "space", 1)
    grad_strip = grad_extended[:, 5 : strip_rows + 5]
    grad_strip = grad_strip.at[:, strip_rows - 5 :].add(from_below).at[:, 0:5].add(from_above)
    grad_received = pull_owner(grad_strip)[0]
    returned = lax.all_to_all(grad_received, "space", split_axis=0, concat_axis=0, tiled=True)
    grad_records = pull_sender(returned)[0]
    grad_params = lax.psum(pull_project(grad_records)[0], "view")
    loss_sum = lax.psum(own_loss, "space")
    loss_value = (loss_sum / (3.0 * height_px * width_px)).reshape(1)
    return (grad_params, strip[None], loss_value)


def solution(mesh):
    in_specs = (
        P(None, "space"),
        P("space", None, None),
        P("space", None),
        P("space", None),
        P("view", None),
        P("view", None),
        P("view", None),
        P("view", None, "space", None),
    )
    out_specs = (P(None, "space"), P("view", None, "space", None), P("view"))
    return jax.shard_map(shards, mesh=mesh, in_specs=in_specs, out_specs=out_specs, check_vma=False)
```

profile of v0, /device:TPU:0, one launch (start us, length us, event | category | flops | bytes accessed | tf_op | source)
XLA Modules:
  0.0 244.3 jit_solution(11177102204411708343)
XLA Ops:
  9.9 7.3 %all-to-all-start = ((s32[8,1,16]{2,1,0:T(1,128)}), s32[8,1,16]{2,1,0:T(1,128)S(1)}, u32[]{:S(2)}, u32[]{:S(2)}) async-start(s32[8,1,16]{2,1,0:T(1,128)} %bitcast.45), calls=%async_computation | async-start | bytes 8192 | tf_op jit(solution)/shard_map/all_to_all | solution.py:270
  37.9 0.9 multiply_reduce_fusion.6
  38.9 4.8 %add_divide_fusion = (f32[1,2048]{1,0:T(1,128)S(1)}, f32[1,2048]{1,0:T(1,128)S(1)}, f32[1,2048]{1,0:T(1,128)S(1)}) fusion(f32[59,2048]{1,0:T(8,128)} %param.12, f32[]{:T(128)} %bitcast.50, f32[]{:T(128)} %bitcast.49, f32[]{:T(128)} %bitcast.48, f32[]{:T(128)} %bitcast.53, f32[]{:T(128)} %bitcast.52, f32[]{:T(128)} %bitcast.51), kind=kLoop, calls=%fused_computation.484 | loop fusion | flops 34816 | bytes 57368 | tf_op jit(solution)/shard_map/jvp()/div | solution.py:152
  44.6 1.1 slice.579
  52.8 0.9 slice_divide_fusion
  55.5 4.6 %fusion.269 = (f32[1,2048]{1,0:T(1,128)S(1)}, f32[1,2048]{1,0:T(1,128)S(1)}, f32[1,2048]{1,0:T(1,128)}, f32[1,2048]{1,0:T(1,128)S(1)}, f32[1,2048]{1,0:T(1,128)}...) fusion(f32[3,2048]{1,0:T(4,128)S(1)} %slice_exponential_fusion,, ...), kind=kLoop, calls=%fused_computation.586 | loop fusion | flops 159744 | bytes 213040 | tf_op jit(solution)/shard_map/jvp()/div | solution.py:157
  61.3 5.5 %gather_fusion = f32[2048,9]{1,0:T(8,128)S(1)} fusion(f32[9,2048]{0,1:T(8,128)S(1)} %copy.299, s32[2048]{0:T(1024)S(1)} %broadcast_clamp_fusion), kind=kCustom, calls=%fused_computation | custom fusion | bytes 155648 | tf_op jit(solution)/shard_map/jvp()/gather | solution.py:264
  66.8 0.9 copy.300
  68.6 6.0 %all-to-all-start.1 = ((f32[8,9,256]{2,1,0:T(8,128)}), f32[8,9,256]{2,1,0:T(8,128)S(1)}, u32[]{:S(2)}, u32[]{:S(2)}) async-start(f32[8,9,256]{2,1,0:T(8,128)} %copy.301), calls=%async_computation.1 | async-start | bytes 262144 | tf_op jit(solution)/shard_map/all_to_all | solution.py:269
  75.1 6.9 %all-to-all-done.1 = f32[8,9,256]{2,1,0:T(8,128)S(1)} async-done(((f32[8,9,256]{2,1,0:T(8,128)}), f32[8,9,256]{2,1,0:T(8,128)S(1)}, u32[]{:S(2)}, u32[]{:S(2)}) %all-to-all-start.1) | async-done | bytes 73760 | tf_op jit(solution)/shard_map/all_to_all | solution.py:269
  82.5 1.7 negate_log-plus-one_fusion
  84.6 3.7 %fusion.30 = f32[128,3,128]{2,1,0:T(4,128)S(1)} fusion(f32[3,128,16]{2,0,1:T(4,128)S(1)} %bitcast.204, f32[128,16]{1,0:T(8,128)S(1)} %bitcast.169, f32[128,16,128]{2,0,1:T(8,128)S(1)} %fusion.26, f32[128,16]{1,0:T(8,128)S(1)} %bitcast.174, f32[128,16]{1,0:T(8,128)S(1)} %bitcast.179, f32[128,128]{1,0:T(8,128)S(1)} %get-tuple-element.200, ...), kind=kOutput, calls=%fused_computation.64 | convolution fusion | flops 13631488 | bytes 1449984 | tf_op jit(solution)/shard_map/jvp(skp,csk->scp)/dot_general | solution.py:182
  93.5 2.1 collective-permute-start
  95.6 1.5 collective-permute-start.1
  97.2 1.6 collective-permute-done
  98.8 3.3 %collective-permute-done.1 = f32[6,5,512]{2,1,0:T(8,128)S(1)} collective-permute-done((f32[6,5,512]{2,1,0:T(8,128)S(1)}, f32[6,5,512]{2,1,0:T(8,128)S(1)}, u32[]{:S(2)}, u32[]{:S(2)}) %collective-permute-start.1) | collective-permute-done | bytes 61472 | tf_op jit(solution)/shard_map/ppermute | solution.py:40
  105.2 1.3 add_reduce_fusion
  108.8 1.0 fusion.41
  109.8 1.3 collective-permute-start.2
  111.1 4.8 %collective-permute-start.3 = (f32[3,5,512]{2,1,0:T(8,128)S(1)}, f32[3,5,512]{2,1,0:T(8,128)S(1)}, u32[]{:S(2)}, u32[]{:S(2)}) collective-permute-start(f32[3,5,512]{2,1,0:T(8,128)S(1)} %get-tuple-element.131), channel_id=1, source_target_pairs={{0,4},{4,8},{8,12},{12,16},{16,20},{20,24},{24,28},{1,5},{5,9},{9,... | collective-permute-start | bytes 92168 | tf_op jit(solution)/shard_map/ppermute | solution.py:48
  116.1 1.3 collective-permute-done.3
  119.6 0.9 copy-done.6
  124.2 4.2 %convolution_bitcast_fusion.1 = f32[3,128,16]{2,0,1:T(4,128)S(1)} fusion(f32[128,16]{1,0:T(8,128)S(1)} %bitcast.170, f32[128,16,128]{2,0,1:T(8,128)S(1)} %copy-done.3, f32[128,3,128]{2,0,1:T(8,128)S(1)} %split.13, f32[128,16]{1,0:T(8,128)S(1)} %bitcast.175, f32[128,16]{1,0:T(8,128)S(1)} %bitcast.180, f32[128,128]{1,0:T(8,128)S(1)} %copy-done.18, ...), kind=kOutput, calls=%fused_computation.18 | convolution fusion | flops 13631488 | bytes 1449984 | tf_op jit(solution)/shard_map/transpose(jvp(skp,csk->scp))/dot_general | solution.py:182
  128.4 4.0 %multiply_multiply_fusion = (f32[128,16,128]{2,1,0:T(8,128)S(1)}, f32[128,16,128]{2,1,0:T(8,128)S(1)}) fusion(f32[128,16]{1,0:T(8,128)S(1)} %bitcast.171, f32[128,16,128]{2,0,1:T(8,128)S(1)} %copy-done.3, f32[128,16]{1,0:T(8,128)S(1)} %bitcast.176, f32[128,16]{1,0:T(8,128)S(1)} %bitcast.181, f32[128,128]{1,0:T(8,128)S(1)} %copy-done.18, ...), kind=kOutput, calls=%fused_computation.50 | convolution fusion | flops 13893632 | bytes 3547136 | tf_op jit(solution)/shard_map/transpose(jvp(skp,csk->scp))/dot_general | solution.py:182
  132.7 5.5 %fusion.15 = (f32[128,16]{1,0:T(8,128)S(1)}, f32[128,16]{1,0:T(8,128)S(1)}, f32[128,16]{1,0:T(8,128)S(1)}, f32[128,16]{1,0:T(8,128)S(1)}, f32[128,16]{1,0:T(8,128)S(1)}, /*index=5*/f32[128,16]{1,0:T(8,128)S(1)}) fusion(f32[128,16]{1,0:T(8,128)S(1)} %bitcast.182, f32[128,128]{1,0:T(8,128)S(1)} %copy-done.18, f32[128,16]{1,0:T(8,128)S(1)} %bitcast.177, ...), kind=kLoop, calls=%fused_computation.32 | loop fusion | flops 13357056 | bytes 3440640 | tf_op jit(solution)/shard_map/transpose(jvp())/reduce_sum | solution.py:176
  140.3 6.8 %all-to-all-start.2 = ((f32[8,9,256]{2,1,0:T(8,128)}), f32[8,9,256]{2,1,0:T(8,128)S(1)}, u32[]{:S(2)}, u32[]{:S(2)}) async-start(f32[8,9,256]{2,1,0:T(8,128)} %copy.321), calls=%async_computation.2 | async-start | bytes 262144 | tf_op jit(solution)/shard_map/all_to_all | solution.py:301
  147.8 6.6 %all-to-all-done.2 = f32[8,9,256]{2,1,0:T(8,128)S(1)} async-done(((f32[8,9,256]{2,1,0:T(8,128)}), f32[8,9,256]{2,1,0:T(8,128)S(1)}, u32[]{:S(2)}, u32[]{:S(2)}) %all-to-all-start.2) | async-done | bytes 73760 | tf_op jit(solution)/shard_map/all_to_all | solution.py:301
  154.7 1.8 copy.352
  156.5 12.3 %scatter_custom_fusion = f32[9,2048]{0,1:T(8,128)S(1)} fusion(s32[2048]{0:T(1024)} %copy-done.36, f32[2048,9]{1,0:T(8,128)} %bitcast.166, f32[]{:T(128)} %constant.222.clone.1), kind=kCustom, calls=%fused_computation.61 | custom fusion | flops 18432 | bytes 74240 | tf_op jit(solution)/shard_map/transpose(jvp())/scatter-add | solution.py:264
  168.8 1.3 split.15
  170.2 3.7 %fusion.270 = (f32[1,2048]{0,1:T(8,128)}, f32[1,2048]{0,1:T(8,128)}, f32[1,2048]{0,1:T(8,128)}, f32[1,2048]{0,1:T(8,128)}, f32[1,2048]{0,1:T(8,128)S(1)}, /*index=5*/f32[1,2048]{0,1:T(8,128)}) fusion(f32[9,2048]{0,1:T(8,128)S(1)} %scatter_custom_fusion), kind=kLoop, calls=%fused_computation.587 | loop fusion | bytes 98304 | tf_op jit(solution)/shard_map/transpose(jvp())/unstack | solution.py:156
  173.9 1.6 copy.324
  175.6 0.9 broadcast_in_dim.33
  176.5 1.6 copy.354
  178.4 1.7 copy.359
  180.1 1.6 copy.357
  183.3 4.0 %add_add_fusion.6 = (f32[1,2048]{1,0:T(1,128)S(1)}, f32[1,2048]{1,0:T(1,128)S(1)}, f32[1,2048]{1,0:T(1,128)S(1)}, f32[1,2048]{1,0:T(1,128)S(1)}, f32[1,2048]{1,0...) fusion(f32[4,2048]{1,0:T(4,128)S(1)} %slice_divide_fusion, ...), kind=kLoop, calls=%fused_computation.445 | loop fusion | flops 167936 | bytes 237592 | tf_op jit(solution)/shard_map/transpose(jvp())/add_any | solution.py:113
  187.4 2.5 %multiply_add_fusion.8 = f32[1,2048]{1,0:T(1,128)S(1)} fusion(f32[1,2048]{1,0:T(1,128)S(1)} %get-tuple-element.62, f32[1,2048]{1,0:T(1,128)S(1)} %get-tuple-element.67, f32[1,2048]{1,0:T(1,128)S(1)} %get-tuple-element.66, f32[1,2048]{1,0:T(1,128)S(1)} %get-tuple-element.63, f32[1,2048]{1,0:T(1,128)S(1)} %get-tuple-element.65, ...), kind=kLoop, calls=%fused_computation.469 | loop fusion | flops 65536 | bytes 139280 | tf_op jit(solution)/shard_map/transpose(jvp())/add_any | solution.py:114
  189.9 2.7 %add_add_fusion.5 = f32[1,2048]{1,0:T(1,128)S(1)} fusion(f32[1,2048]{1,0:T(1,128)S(1)} %get-tuple-element.62, f32[1,2048]{1,0:T(1,128)S(1)} %get-tuple-element.67, f32[1,2048]{1,0:T(1,128)S(1)} %get-tuple-element.66, f32[1,2048]{1,0:T(1,128)S(1)} %get-tuple-element.64, f32[1,2048]{1,0:T(1,128)S(1)} %get-tuple-element.65, ...), kind=kLoop, calls=%fused_computation.444 | loop fusion | flops 65536 | bytes 139280 | tf_op jit(solution)/shard_map/transpose(jvp())/add_any | solution.py:113
  194.7 1.0 multiply_reduce_fusion.5
  196.4 1.0 add_add_fusion.3
  197.5 3.8 %multiply_add_fusion.12 = (f32[1,2048]{1,0:T(1,128)S(1)}, f32[1,2048]{1,0:T(1,128)S(1)}, f32[1,2048]{1,0:T(1,128)S(1)}, f32[1,2048]{1,0:T(1,128)S(1)}) fusion(f32[1,2048]{1,0:T(1,128)S(1)} %copy.356, f32[1,2048]{1,0:T(1,128)S(1)} %copy.355, f32[]{:T(128)} %bitcast.52, f32[]{:T(128)} %bitcast.49, f32[]{:T(128)} %bitcast.48, f32[]{:T(128)} %bitcast.51, ...), kind=kLoop, calls=%fused_computation.483 | loop fusion | flops 16384 | bytes 49176 | tf_op jit(solution)/shard_map/transpose(jvp())/add_any | solution.py:150
  201.3 0.9 add_multiply_fusion.1
  202.2 0.9 pad_add_fusion.1
  203.1 1.0 reshape.522
  204.2 18.8 %psum.15 = f32[]{:T(128)} all-reduce(f32[]{:T(128)} %get-tuple-element.56), channel_id=1, replica_groups=mesh['space'=8,'view'=4] {'space'}, use_global_device_ids=true, to_apply=%region_17.18 | all-reduce | flops 1 | bytes 8 | tf_op jit(solution)/shard_map/psum | solution.py:304
  223.7 10.8 %all-reduce.101.cloned.1.call-done = f32[59,2048]{1,0:T(8,128)} async-done(((f32[59,2048]{1,0:T(8,128)}), f32[59,2048]{1,0:T(8,128)}) %all-reduce.101.cloned.1.call-update) | async-done | bytes 483344 | tf_op jit(solution)/shard_map/psum | solution.py:303
  234.5 1.9 copy.406
  (255 shorter events, 37.6 us)
Async XLA Ops:
  9.9 58.7 %all-to-all-start = ((s32[8,1,16]{2,1,0:T(1,128)}), s32[8,1,16]{2,1,0:T(1,128)S(1)}, u32[]{:S(2)}, u32[]{:S(2)}) async-start(s32[8,1,16]{2,1,0:T(1,128)} %bitcast.45), calls=%async_computation | async-start | bytes 8192 | tf_op jit(solution)/shard_map/all_to_all | solution.py:270
  38.9 13.3 %copy-start.31 = (f32[2048]{0:T(1024)}, f32[2048]{0:T(1024)S(1)}, u32[]{:S(2)}) copy-start(f32[2048]{0:T(1024)S(1)} %multiply_reduce_fusion.6) | copy-start | bytes 24580
  43.7 17.0 %copy-start.33 = (f32[1,2048]{1,0:T(1,128)}, f32[1,2048]{1,0:T(1,128)S(1)}, u32[]{:S(2)}) copy-start(f32[1,2048]{1,0:T(1,128)S(1)} %get-tuple-element.121) | copy-start | bytes 24580
  50.8 1.3 copy-start.52
  52.8 0.9 copy-start.29
  68.6 19.8 %copy-start.27 = (s32[8,1,16]{2,1,0:T(1,128)}, s32[8,1,16]{2,1,0:T(1,128)S(1)}, u32[]{:S(2)}) copy-start(s32[8,1,16]{2,1,0:T(1,128)S(1)} %all-to-all-done) | copy-start | bytes 1540
  68.6 13.3 %all-to-all-start.1 = ((f32[8,9,256]{2,1,0:T(8,128)}), f32[8,9,256]{2,1,0:T(8,128)S(1)}, u32[]{:S(2)}, u32[]{:S(2)}) async-start(f32[8,9,256]{2,1,0:T(8,128)} %copy.301), calls=%async_computation.1 | async-start | bytes 262144 | tf_op jit(solution)/shard_map/all_to_all | solution.py:269
  75.0 9.5 %copy-start.17 = (f32[128,128]{1,0:T(8,128)}, f32[128,128]{1,0:T(8,128)S(1)}, u32[]{:S(2)}) copy-start(f32[128,128]{1,0:T(8,128)S(1)} %get-tuple-element.200) | copy-start | bytes 196612
  75.0 9.5 %copy-start.19 = (f32[128,128]{1,0:T(8,128)}, f32[128,128]{1,0:T(8,128)S(1)}, u32[]{:S(2)}) copy-start(f32[128,128]{1,0:T(8,128)S(1)} %get-tuple-element.201) | copy-start | bytes 196612
  82.3 2.3 copy-start.7
  82.3 2.3 copy-start.9
  82.3 2.3 copy-start.11
  82.3 2.3 copy-start.13
  82.3 2.3 copy-start.15
  82.5 2.2 copy-start.23
  84.5 3.8 %copy-start.2 = (f32[128,16,128]{2,0,1:T(8,128)}, f32[128,16,128]{2,0,1:T(8,128)S(1)}, u32[]{:S(2)}) copy-start(f32[128,16,128]{2,0,1:T(8,128)S(1)} %fusion.26) | copy-start | bytes 3145732
  92.6 0.9 copy-start.5
  93.5 5.3 %collective-permute-start = (f32[6,5,512]{2,1,0:T(8,128)S(1)}, f32[6,5,512]{2,1,0:T(8,128)S(1)}, u32[]{:S(2)}, u32[]{:S(2)}) collective-permute-start(f32[6,5,512]{2,1,0:T(8,128)S(1)} %get-tuple-element.148), channel_id=1, source_target_pairs={{0,4},{4,8},{8,12},{12,16},{16,20},{20,24},{24,28},{1,5},{5,9},{9,... | collective-permute-start | bytes 184328 | tf_op jit(solution)/shard_map/ppermute | solution.py:39
  95.6 6.5 %collective-permute-start.1 = (f32[6,5,512]{2,1,0:T(8,128)S(1)}, f32[6,5,512]{2,1,0:T(8,128)S(1)}, u32[]{:S(2)}, u32[]{:S(2)}) collective-permute-start(f32[6,5,512]{2,1,0:T(8,128)S(1)} %get-tuple-element.149), channel_id=1, source_target_pairs={{4,0},{8,4},{12,8},{16,12},{20,16},{24,20},{28,24},{5,1},{9,5},{13... | collective-permute-start | bytes 184328 | tf_op jit(solution)/shard_map/ppermute | solution.py:40
  109.8 6.1 %collective-permute-start.2 = (f32[3,5,512]{2,1,0:T(8,128)S(1)}, f32[3,5,512]{2,1,0:T(8,128)S(1)}, u32[]{:S(2)}, u32[]{:S(2)}) collective-permute-start(f32[3,5,512]{2,1,0:T(8,128)S(1)} %get-tuple-element.132), channel_id=1, source_target_pairs={{4,0},{8,4},{12,8},{16,12},{20,16},{24,20},{28,24},{5,1},{9,5},{13... | collective-permute-start | bytes 92168 | tf_op jit(solution)/shard_map/ppermute | solution.py:48
  111.1 6.3 %collective-permute-start.3 = (f32[3,5,512]{2,1,0:T(8,128)S(1)}, f32[3,5,512]{2,1,0:T(8,128)S(1)}, u32[]{:S(2)}, u32[]{:S(2)}) collective-permute-start(f32[3,5,512]{2,1,0:T(8,128)S(1)} %get-tuple-element.131), channel_id=1, source_target_pairs={{0,4},{4,8},{8,12},{12,16},{16,20},{20,24},{24,28},{1,5},{5,9},{9,... | collective-permute-start | bytes 92168 | tf_op jit(solution)/shard_map/ppermute | solution.py:48
  119.5 1.0 copy-start.6
  120.4 1.1 copy-start.51
  120.7 0.8 copy-start.22
  122.6 1.2 copy-start.3
  122.6 1.2 copy-start.20
  123.2 0.9 copy-start.8
  123.2 0.9 copy-start.10
  123.2 0.9 copy-start.12
  123.2 1.0 copy-start.14
  123.2 1.0 copy-start.16
  123.2 1.0 copy-start.18
  124.2 4.2 %copy-start.24 = (f32[3,8,16,16]{3,0,2,1:T(4,128)S(1)}, f32[3,8,16,16]{3,0,2,1:T(4,128)}, u32[]{:S(2)}) copy-start(f32[3,8,16,16]{3,0,2,1:T(4,128)} %copy-done.23) | copy-start | bytes 73732
  140.3 6.8 %copy-start.54 = (f32[16]{0:T(128)S(1)}, f32[16]{0:T(128)}, u32[]{:S(2)}) copy-start(f32[16]{0:T(128)} %copy-done.53) | copy-start | bytes 196
  140.3 14.1 %all-to-all-start.2 = ((f32[8,9,256]{2,1,0:T(8,128)}), f32[8,9,256]{2,1,0:T(8,128)S(1)}, u32[]{:S(2)}, u32[]{:S(2)}) async-start(f32[8,9,256]{2,1,0:T(8,128)} %copy.321), calls=%async_computation.2 | async-start | bytes 262144 | tf_op jit(solution)/shard_map/all_to_all | solution.py:301
  147.1 87.4 %all-reduce.101.cloned.1.call-start = ((), (), s32[]{:S(2)}) async-start(), calls=%async_computation.3 | async-start | bytes 1048576 | tf_op jit(solution)/shard_map/psum | solution.py:303
  175.6 2.6 %copy-start.1 = (f32[1,2048]{0,1:T(8,128)S(1)}, f32[1,2048]{0,1:T(8,128)}, u32[]{:S(2)}) copy-start(f32[1,2048]{0,1:T(8,128)} %get-tuple-element.106) | copy-start | bytes 24580
  176.5 1.6 copy-start.34
  178.4 3.4 %copy-start = (f32[1,2048]{0,1:T(8,128)S(1)}, f32[1,2048]{0,1:T(8,128)}, u32[]{:S(2)}) copy-start(f32[1,2048]{0,1:T(8,128)} %get-tuple-element.108) | copy-start | bytes 24580
  180.1 1.6 copy-start.26
  180.1 1.6 copy-start.43
  182.2 5.1 %copy-start.42 = (f32[1,2048]{1,0:T(1,128)S(1)}, f32[1,2048]{1,0:T(1,128)}, u32[]{:S(2)}) copy-start(f32[1,2048]{1,0:T(1,128)} %get-tuple-element.100) | copy-start | bytes 24580
  182.2 5.1 %copy-start.41 = (f32[1,2048]{1,0:T(1,128)S(1)}, f32[1,2048]{1,0:T(1,128)}, u32[]{:S(2)}) copy-start(f32[1,2048]{1,0:T(1,128)} %get-tuple-element.102) | copy-start | bytes 24580
  182.2 7.7 %copy-start.40 = (f32[1,2048]{1,0:T(1,128)S(1)}, f32[1,2048]{1,0:T(1,128)}, u32[]{:S(2)}) copy-start(f32[1,2048]{1,0:T(1,128)} %get-tuple-element.95) | copy-start | bytes 24580
  187.2 10.1 %copy-start.4 = (f32[48,2048]{1,0:T(8,128)S(1)}, f32[48,2048]{1,0:T(8,128)}, u32[]{:S(2)}) copy-start(f32[48,2048]{1,0:T(8,128)} %broadcast_in_dim.33) | copy-start | bytes 1179652
  189.9 2.7 %copy-start.39 = (f32[1,2048]{1,0:T(1,128)S(1)}, f32[1,2048]{1,0:T(1,128)}, u32[]{:S(2)}) copy-start(f32[1,2048]{1,0:T(1,128)} %get-tuple-element.98) | copy-start | bytes 24580
  194.7 1.0 copy-start.32
  196.4 1.0 copy-start.57
  (23 other events, 15.4 us)
Sparse Core Ops, SparseCore 0:
  203.3 31.1 all-reduce.100
where the time goes:
time: 246 us; the launch traced here: 244 us
  other arithmetic  61 us (25%)
  local copies, waits for them, and re-layouts  49.4 us (20%)
  between operations  40.5 us (16%)
  waiting for transfers between devices  30.6 us (12%)
  starting transfers between devices  29.8 us (12%)
  blocking collectives  18.8 us (8%)
  matrix products  14.2 us (6%)
    unnamed x135, local copies, waits for them, and re-layouts  21.7 us
    psum x1, blocking collectives, shards(): loss_sum = lax.psum(own_loss, 'space')  18.8 us
    scatter-add x1, other arithmetic, sender_side(): picked = record_in[:, lists]  12.3 us
    dot_general x3, matrix products, render(): jnp.einsum('skp,csk->scp', weights, gathered[6:9], precision=HIGHEST)  11.8 us
    psum x1, waiting for transfers between devices, shards(): grad_params = lax.psum(pull_project(grad_records)[0], 'view')  10.8 us
    all_to_all x1, starting transfers between devices, shards(): lax.all_to_all(target_ids, 'space', split_axis=0, concat_axis=0, tiled=True)  7.31 us
    all_to_all x1, waiting for transfers between devices, shards(): lax.all_to_all(message, 'space', split_axis=0, concat_axis=0, tiled=True)  6.88 us
    all_to_all x1, starting transfers between devices, shards(): lax.all_to_all(grad_received, 'space', split_axis=0, concat_axis=0, tiled...  6.8 us
  transfers between devices with their start and end apart: 8, of which 6 were waited for; matrix products, arithmetic and copies ran while one was open for 11% of the time, Pallas kernels for 0%

commit v1 on v0

--- a/solution.py
+++ b/solution.py
@@ -300,7 +300,7 @@
     grad_received = pull_owner(grad_strip)[0]
     returned = lax.all_to_all(grad_received, "space", split_axis=0, concat_axis=0, tiled=True)
     grad_records = pull_sender(returned)[0]
-    grad_params = lax.psum(pull_project(grad_records)[0], "view")
+    grad_params = lax.all_gather(pull_project(grad_records)[0], axis_name="view").sum(axis=0)
     loss_sum = lax.psum(own_loss, "space")
     loss_value = (loss_sum / (3.0 * height_px * width_px)).reshape(1)
     return (grad_params, strip[None], loss_value)

time: 246 us -> 234 us (0.951)
  local copies, waits for them, and re-layouts: 49.4 us -> 37 us
  waiting for transfers between devices: 30.6 us -> 19.8 us
  other arithmetic: 61 us -> 70.8 us
    unnamed x135 -> x88, local copies, waits for them, and re-layouts: 21.7 us -> 9.24 us
    psum x1 -> x0, waiting for transfers between devices: 10.8 us -> none  [shards(): grad_params = lax.psum(pull_project(grad_records)[0], 'view')]
    mul x6, other arithmetic: 0.07 us -> 2.86 us  [project(): (turn[row, 0] * spin[0][col] + turn[row, 1] * spin[1][col] + turn[row, 2]...]
    reduce_sum x0 -> x1, other arithmetic: none -> 2.56 us  [shards(): lax.all_gather(pull_project(grad_records)[0], axis_name='view').sum(axis=0)]
  transfers between devices with their start and end apart: 8 -> 8, of which waited for: 6 -> 5; matrix products, arithmetic and copies ran while one was open for 11% -> 13% of each run, Pallas kernels for 0% -> 0%
where the time goes in v1:
time: 234 us; the launch traced here: 232 us
  other arithmetic  70.8 us (30%)
  between operations  40.6 us (17%)
  local copies, waits for them, and re-layouts  37 us (16%)
  starting transfers between devices  29.7 us (13%)
  waiting for transfers between devices  19.8 us (8%)
  blocking collectives  18.8 us (8%)
  matrix products  15.6 us (7%)
    psum x1, blocking collectives, shards(): loss_sum = lax.psum(own_loss, 'space')  18.8 us
    scatter-add x1, other arithmetic, sender_side(): picked = record_in[:, lists]  12.3 us
    dot_general x3, matrix products, render(): jnp.einsum('skp,csk->scp', weights, gathered[6:9], precision=HIGHEST)  11.8 us
    unnamed x88, local copies, waits for them, and re-layouts  9.24 us
    all_to_all x1, starting transfers between devices, shards(): lax.all_to_all(target_ids, 'space', split_axis=0, concat_axis=0, tiled=True)  7.31 us
    all_to_all x1, waiting for transfers between devices, shards(): lax.all_to_all(message, 'space', split_axis=0, concat_axis=0, tiled=True)  6.88 us
    all_to_all x1, starting transfers between devices, shards(): lax.all_to_all(grad_received, 'space', split_axis=0, concat_axis=0, tiled...  6.67 us
    all_to_all x1, waiting for transfers between devices, shards(): lax.all_to_all(grad_received, 'space', split_axis=0, concat_axis=0, tiled...  6.59 us
  transfers between devices with their start and end apart: 8, of which 5 were waited for; matrix products, arithmetic and copies ran while one was open for 13% of the time, Pallas kernels for 0%

profile of v1, /device:TPU:0, one launch (start us, length us, event | category | flops | bytes accessed | tf_op | source)
XLA Modules:
  0.0 232.3 jit_solution(13551380403058516265)
XLA Ops:
  7.7 1.3 reduce.24
  9.1 1.3 fusion.221
  10.4 7.3 %all-to-all-start = ((s32[8,1,16]{2,1,0:T(1,128)}), s32[8,1,16]{2,1,0:T(1,128)S(1)}, u32[]{:S(2)}, u32[]{:S(2)}) async-start(s32[8,1,16]{2,1,0:T(1,128)} %bitcast.45), calls=%async_computation | async-start | bytes 8192 | tf_op jit(solution)/shard_map/all_to_all | solution.py:270
  17.7 1.4 fusion.275
  38.8 0.9 multiply_reduce_fusion.6
  39.7 4.8 %add_divide_fusion = (f32[1,2048]{1,0:T(1,128)S(1)}, f32[1,2048]{1,0:T(1,128)S(1)}, f32[1,2048]{1,0:T(1,128)S(1)}) fusion(f32[59,2048]{1,0:T(8,128)} %param.12, f32[]{:T(128)} %bitcast.50, f32[]{:T(128)} %bitcast.49, f32[]{:T(128)} %bitcast.48, f32[]{:T(128)} %bitcast.53, f32[]{:T(128)} %bitcast.52, f32[]{:T(128)} %bitcast.51), kind=kLoop, calls=%fused_computation.484 | loop fusion | flops 34816 | bytes 57368 | tf_op jit(solution)/shard_map/jvp()/div | solution.py:152
  45.3 1.1 slice.579
  54.2 0.9 slice_divide_fusion
  56.4 4.6 %fusion.269 = (f32[1,2048]{1,0:T(1,128)S(1)}, f32[1,2048]{1,0:T(1,128)S(1)}, f32[1,2048]{1,0:T(1,128)}, f32[1,2048]{1,0:T(1,128)S(1)}, f32[1,2048]{1,0:T(1,128)}...) fusion(f32[3,2048]{1,0:T(4,128)S(1)} %slice_exponential_fusion,, ...), kind=kLoop, calls=%fused_computation.586 | loop fusion | flops 159744 | bytes 213040 | tf_op jit(solution)/shard_map/jvp()/div | solution.py:157
  61.6 5.5 %gather_fusion = f32[2048,9]{1,0:T(8,128)S(1)} fusion(f32[9,2048]{0,1:T(8,128)S(1)} %copy.301, s32[2048]{0:T(1024)S(1)} %broadcast_clamp_fusion), kind=kCustom, calls=%fused_computation | custom fusion | bytes 155648 | tf_op jit(solution)/shard_map/jvp()/gather | solution.py:264
  68.9 6.0 %all-to-all-start.1 = ((f32[8,9,256]{2,1,0:T(8,128)}), f32[8,9,256]{2,1,0:T(8,128)S(1)}, u32[]{:S(2)}, u32[]{:S(2)}) async-start(f32[8,9,256]{2,1,0:T(8,128)} %copy.303), calls=%async_computation.1 | async-start | bytes 262144 | tf_op jit(solution)/shard_map/all_to_all | solution.py:269
  75.4 6.9 %all-to-all-done.1 = f32[8,9,256]{2,1,0:T(8,128)S(1)} async-done(((f32[8,9,256]{2,1,0:T(8,128)}), f32[8,9,256]{2,1,0:T(8,128)S(1)}, u32[]{:S(2)}, u32[]{:S(2)}) %all-to-all-start.1) | async-done | bytes 73760 | tf_op jit(solution)/shard_map/all_to_all | solution.py:269
  82.8 1.7 negate_log-plus-one_fusion
  84.9 3.7 %fusion.30 = f32[128,3,128]{2,1,0:T(4,128)S(1)} fusion(f32[3,128,16]{2,0,1:T(4,128)S(1)} %bitcast.206, f32[128,16]{1,0:T(8,128)S(1)} %bitcast.171, f32[128,16,128]{2,0,1:T(8,128)S(1)} %fusion.26, f32[128,16]{1,0:T(8,128)S(1)} %bitcast.176, f32[128,16]{1,0:T(8,128)S(1)} %bitcast.181, f32[128,128]{1,0:T(8,128)S(1)} %get-tuple-element.191, ...), kind=kOutput, calls=%fused_computation.64 | convolution fusion | flops 13631488 | bytes 1449984 | tf_op jit(solution)/shard_map/jvp(skp,csk->scp)/dot_general | solution.py:182
  91.4 2.1 collective-permute-start
  93.6 1.5 collective-permute-start.1
  95.1 1.6 collective-permute-done
  96.8 3.3 %collective-permute-done.1 = f32[6,5,512]{2,1,0:T(8,128)S(1)} collective-permute-done((f32[6,5,512]{2,1,0:T(8,128)S(1)}, f32[6,5,512]{2,1,0:T(8,128)S(1)}, u32[]{:S(2)}, u32[]{:S(2)}) %collective-permute-start.1) | collective-permute-done | bytes 61472 | tf_op jit(solution)/shard_map/ppermute | solution.py:40
  103.2 1.3 add_reduce_fusion
  106.7 1.0 fusion.41
  107.7 1.3 collective-permute-start.2
  109.1 4.8 %collective-permute-start.3 = (f32[3,5,512]{2,1,0:T(8,128)S(1)}, f32[3,5,512]{2,1,0:T(8,128)S(1)}, u32[]{:S(2)}, u32[]{:S(2)}) collective-permute-start(f32[3,5,512]{2,1,0:T(8,128)S(1)} %get-tuple-element.122), channel_id=1, source_target_pairs={{0,4},{4,8},{8,12},{12,16},{16,20},{20,24},{24,28},{1,5},{5,9},{9,... | collective-permute-start | bytes 92168 | tf_op jit(solution)/shard_map/ppermute | solution.py:48
  114.1 1.3 collective-permute-done.3
  115.9 1.5 multiply_reduce_fusion.3
  120.8 4.2 %convolution_bitcast_fusion.1 = f32[3,128,16]{2,0,1:T(4,128)S(1)} fusion(f32[128,16]{1,0:T(8,128)S(1)} %bitcast.172, f32[128,16,128]{2,0,1:T(8,128)S(1)} %copy-done.2, f32[128,3,128]{2,0,1:T(8,128)S(1)} %split.13, f32[128,16]{1,0:T(8,128)S(1)} %bitcast.177, f32[128,16]{1,0:T(8,128)S(1)} %bitcast.182, f32[128,128]{1,0:T(8,128)S(1)} %copy-done.12, ...), kind=kOutput, calls=%fused_computation.18 | convolution fusion | flops 13631488 | bytes 1449984 | tf_op jit(solution)/shard_map/transpose(jvp(skp,csk->scp))/dot_general | solution.py:182
  125.0 4.0 %multiply_multiply_fusion = (f32[128,16,128]{2,1,0:T(8,128)S(1)}, f32[128,16,128]{2,1,0:T(8,128)S(1)}) fusion(f32[128,16]{1,0:T(8,128)S(1)} %bitcast.173, f32[128,16,128]{2,0,1:T(8,128)S(1)} %copy-done.2, f32[128,16]{1,0:T(8,128)S(1)} %bitcast.178, f32[128,16]{1,0:T(8,128)S(1)} %bitcast.183, f32[128,128]{1,0:T(8,128)S(1)} %copy-done.12, ...), kind=kOutput, calls=%fused_computation.50 | convolution fusion | flops 13893632 | bytes 3547136 | tf_op jit(solution)/shard_map/transpose(jvp(skp,csk->scp))/dot_general | solution.py:182
  129.3 5.5 %fusion.15 = (f32[128,16]{1,0:T(8,128)S(1)}, f32[128,16]{1,0:T(8,128)S(1)}, f32[128,16]{1,0:T(8,128)S(1)}, f32[128,16]{1,0:T(8,128)S(1)}, f32[128,16]{1,0:T(8,128)S(1)}, /*index=5*/f32[128,16]{1,0:T(8,128)S(1)}) fusion(f32[128,16]{1,0:T(8,128)S(1)} %bitcast.184, f32[128,128]{1,0:T(8,128)S(1)} %copy-done.12, f32[128,16]{1,0:T(8,128)S(1)} %bitcast.179, ...), kind=kLoop, calls=%fused_computation.32 | loop fusion | flops 13357056 | bytes 3440640 | tf_op jit(solution)/shard_map/transpose(jvp())/reduce_sum | solution.py:176
  136.9 6.7 %all-to-all-start.2 = ((f32[8,9,256]{2,1,0:T(8,128)}), f32[8,9,256]{2,1,0:T(8,128)S(1)}, u32[]{:S(2)}, u32[]{:S(2)}) async-start(f32[8,9,256]{2,1,0:T(8,128)} %copy.323), calls=%async_computation.2 | async-start | bytes 262144 | tf_op jit(solution)/shard_map/all_to_all | solution.py:301
  144.3 6.6 %all-to-all-done.2 = f32[8,9,256]{2,1,0:T(8,128)S(1)} async-done(((f32[8,9,256]{2,1,0:T(8,128)}), f32[8,9,256]{2,1,0:T(8,128)S(1)}, u32[]{:S(2)}, u32[]{:S(2)}) %all-to-all-start.2) | async-done | bytes 73760 | tf_op jit(solution)/shard_map/all_to_all | solution.py:301
  151.2 1.8 copy.356
  153.0 12.3 %scatter_custom_fusion = f32[9,2048]{0,1:T(8,128)S(1)} fusion(s32[2048]{0:T(1024)} %copy-done.30, f32[2048,9]{1,0:T(8,128)} %bitcast.168, f32[]{:T(128)} %constant.222.clone.1), kind=kCustom, calls=%fused_computation.61 | custom fusion | flops 18432 | bytes 74240 | tf_op jit(solution)/shard_map/transpose(jvp())/scatter-add | solution.py:264
  165.3 1.4 split.15
  166.7 3.7 %fusion.270 = (f32[1,2048]{0,1:T(8,128)}, f32[1,2048]{0,1:T(8,128)}, f32[1,2048]{0,1:T(8,128)}, f32[1,2048]{0,1:T(8,128)}, f32[1,2048]{0,1:T(8,128)S(1)}, /*index=5*/f32[1,2048]{0,1:T(8,128)}) fusion(f32[9,2048]{0,1:T(8,128)S(1)} %scatter_custom_fusion), kind=kLoop, calls=%fused_computation.587 | loop fusion | bytes 98304 | tf_op jit(solution)/shard_map/transpose(jvp())/unstack | solution.py:156
  170.4 1.6 copy.326
  172.3 1.6 copy.359
  174.0 1.6 copy.363
  175.5 1.6 copy.364
  177.2 1.6 copy.362
  180.2 4.7 %add_add_fusion.6 = (f32[1,2048]{1,0:T(1,128)S(1)}, f32[1,2048]{1,0:T(1,128)S(1)}, f32[1,2048]{1,0:T(1,128)S(1)}, f32[1,2048]{1,0:T(1,128)S(1)}, f32[1,2048]{1,0...) fusion(f32[4,2048]{1,0:T(4,128)S(1)} %slice_divide_fusion, ...), kind=kLoop, calls=%fused_computation.445 | loop fusion | flops 167936 | bytes 237592 | tf_op jit(solution)/shard_map/transpose(jvp())/add_any | solution.py:113
  185.0 2.5 %multiply_add_fusion.8 = f32[1,2048]{1,0:T(1,128)S(1)} fusion(f32[1,2048]{1,0:T(1,128)S(1)} %get-tuple-element.53, f32[1,2048]{1,0:T(1,128)S(1)} %get-tuple-element.58, f32[1,2048]{1,0:T(1,128)S(1)} %get-tuple-element.57, f32[1,2048]{1,0:T(1,128)S(1)} %get-tuple-element.54, f32[1,2048]{1,0:T(1,128)S(1)} %get-tuple-element.56, ...), kind=kLoop, calls=%fused_computation.469 | loop fusion | flops 65536 | bytes 139280 | tf_op jit(solution)/shard_map/transpose(jvp())/add_any | solution.py:114
  188.2 2.6 %add_add_fusion.5 = f32[1,2048]{1,0:T(1,128)S(1)} fusion(f32[1,2048]{1,0:T(1,128)S(1)} %get-tuple-element.53, f32[1,2048]{1,0:T(1,128)S(1)} %get-tuple-element.58, f32[1,2048]{1,0:T(1,128)S(1)} %get-tuple-element.57, f32[1,2048]{1,0:T(1,128)S(1)} %get-tuple-element.55, f32[1,2048]{1,0:T(1,128)S(1)} %get-tuple-element.56, ...), kind=kLoop, calls=%fused_computation.444 | loop fusion | flops 65536 | bytes 139280 | tf_op jit(solution)/shard_map/transpose(jvp())/add_any | solution.py:113
  192.9 1.0 multiply_reduce_fusion.5
  193.9 1.0 add_add_fusion.3
  195.6 3.7 %multiply_add_fusion.12 = (f32[1,2048]{1,0:T(1,128)S(1)}, f32[1,2048]{1,0:T(1,128)S(1)}, f32[1,2048]{1,0:T(1,128)S(1)}, f32[1,2048]{1,0:T(1,128)S(1)}) fusion(f32[1,2048]{1,0:T(1,128)S(1)} %copy.361, f32[1,2048]{1,0:T(1,128)S(1)} %copy.360, f32[]{:T(128)} %bitcast.52, f32[]{:T(128)} %bitcast.49, f32[]{:T(128)} %bitcast.48, f32[]{:T(128)} %bitcast.51, ...), kind=kLoop, calls=%fused_computation.483 | loop fusion | flops 16384 | bytes 49176 | tf_op jit(solution)/shard_map/transpose(jvp())/add_any | solution.py:150
  200.3 0.9 add_bitcast_fusion.1
  201.2 1.0 reshape.522
  202.3 18.8 %psum.7 = f32[]{:T(128)} all-reduce(f32[]{:T(128)} %get-tuple-element.47), channel_id=1, replica_groups=mesh['space'=8,'view'=4] {'space'}, use_global_device_ids=true, to_apply=%region_17.18 | all-reduce | flops 1 | bytes 8 | tf_op jit(solution)/shard_map/psum | solution.py:304
  221.8 2.6 %reduce_sum.154 = f32[59,2048]{1,0:T(8,128)} reduce(f32[4,59,2048]{2,1,0:T(8,128)} %all-gather.4.cloned.1.call-done, f32[]{:T(128)} %constant.222.clone.1), dimensions={0}, to_apply=%region_15.16 | reduce | flops 362496 | bytes 2416644 | tf_op jit(solution)/shard_map/reduce_sum | solution.py:303
  (209 shorter events, 31.6 us)
Async XLA Ops:
  10.4 58.5 %all-to-all-start = ((s32[8,1,16]{2,1,0:T(1,128)}), s32[8,1,16]{2,1,0:T(1,128)S(1)}, u32[]{:S(2)}, u32[]{:S(2)}) async-start(s32[8,1,16]{2,1,0:T(1,128)} %bitcast.45), calls=%async_computation | async-start | bytes 8192 | tf_op jit(solution)/shard_map/all_to_all | solution.py:270
  39.7 15.4 %copy-start.25 = (f32[2048]{0:T(1024)}, f32[2048]{0:T(1024)S(1)}, u32[]{:S(2)}) copy-start(f32[2048]{0:T(1024)S(1)} %multiply_reduce_fusion.6) | copy-start | bytes 24580
  44.5 16.5 %copy-start.27 = (f32[1,2048]{1,0:T(1,128)}, f32[1,2048]{1,0:T(1,128)S(1)}, u32[]{:S(2)}) copy-start(f32[1,2048]{1,0:T(1,128)S(1)} %get-tuple-element.112) | copy-start | bytes 24580
  54.2 0.9 copy-start.23
  55.4 11.7 %copy-start.30 = (s32[2048]{0:T(1024)}, s32[2048]{0:T(1024)S(1)}, u32[]{:S(2)}) copy-start(s32[2048]{0:T(1024)S(1)} %reshape.534) | copy-start | bytes 24580
  55.7 0.5 copy-start.37
  61.0 6.1 %copy-start.19 = (f32[1,2048]{1,0:T(1,128)}, f32[1,2048]{1,0:T(1,128)S(1)}, u32[]{:S(2)}) copy-start(f32[1,2048]{1,0:T(1,128)S(1)} %get-tuple-element.87) | copy-start | bytes 24580
  68.9 19.7 %copy-start.21 = (s32[8,1,16]{2,1,0:T(1,128)}, s32[8,1,16]{2,1,0:T(1,128)S(1)}, u32[]{:S(2)}) copy-start(s32[8,1,16]{2,1,0:T(1,128)S(1)} %all-to-all-done) | copy-start | bytes 1540
  68.9 13.3 %all-to-all-start.1 = ((f32[8,9,256]{2,1,0:T(8,128)}), f32[8,9,256]{2,1,0:T(8,128)S(1)}, u32[]{:S(2)}, u32[]{:S(2)}) async-start(f32[8,9,256]{2,1,0:T(8,128)} %copy.303), calls=%async_computation.1 | async-start | bytes 262144 | tf_op jit(solution)/shard_map/all_to_all | solution.py:269
  75.4 9.5 %copy-start.11 = (f32[128,128]{1,0:T(8,128)}, f32[128,128]{1,0:T(8,128)S(1)}, u32[]{:S(2)}) copy-start(f32[128,128]{1,0:T(8,128)S(1)} %get-tuple-element.191) | copy-start | bytes 196612
  75.4 9.5 %copy-start.13 = (f32[128,128]{1,0:T(8,128)}, f32[128,128]{1,0:T(8,128)S(1)}, u32[]{:S(2)}) copy-start(f32[128,128]{1,0:T(8,128)S(1)} %get-tuple-element.192) | copy-start | bytes 196612
  82.6 2.3 copy-start.5
  82.6 2.3 copy-start.7
  82.6 2.3 copy-start.9
  82.8 5.8 %copy-start.17 = (f32[3,8,16,16]{3,0,2,1:T(4,128)}, f32[3,8,16,16]{3,0,2,1:T(4,128)S(1)}, u32[]{:S(2)}) copy-start(f32[3,8,16,16]{3,0,2,1:T(4,128)S(1)} %copy.305) | copy-start | bytes 73732
  84.9 3.8 %copy-start.1 = (f32[128,16,128]{2,0,1:T(8,128)}, f32[128,16,128]{2,0,1:T(8,128)S(1)}, u32[]{:S(2)}) copy-start(f32[128,16,128]{2,0,1:T(8,128)S(1)} %fusion.26) | copy-start | bytes 3145732
  88.6 1.0 copy-start.35
  88.7 1.7 copy-start.39
  89.4 0.6 copy-start.15
  90.1 1.3 copy-start.3
  91.4 5.3 %collective-permute-start = (f32[6,5,512]{2,1,0:T(8,128)S(1)}, f32[6,5,512]{2,1,0:T(8,128)S(1)}, u32[]{:S(2)}, u32[]{:S(2)}) collective-permute-start(f32[6,5,512]{2,1,0:T(8,128)S(1)} %get-tuple-element.139), channel_id=1, source_target_pairs={{0,4},{4,8},{8,12},{12,16},{16,20},{20,24},{24,28},{1,5},{5,9},{9,... | collective-permute-start | bytes 184328 | tf_op jit(solution)/shard_map/ppermute | solution.py:39
  93.6 6.5 %collective-permute-start.1 = (f32[6,5,512]{2,1,0:T(8,128)S(1)}, f32[6,5,512]{2,1,0:T(8,128)S(1)}, u32[]{:S(2)}, u32[]{:S(2)}) collective-permute-start(f32[6,5,512]{2,1,0:T(8,128)S(1)} %get-tuple-element.140), channel_id=1, source_target_pairs={{4,0},{8,4},{12,8},{16,12},{20,16},{24,20},{28,24},{5,1},{9,5},{13... | collective-permute-start | bytes 184328 | tf_op jit(solution)/shard_map/ppermute | solution.py:40
  107.7 6.1 %collective-permute-start.2 = (f32[3,5,512]{2,1,0:T(8,128)S(1)}, f32[3,5,512]{2,1,0:T(8,128)S(1)}, u32[]{:S(2)}, u32[]{:S(2)}) collective-permute-start(f32[3,5,512]{2,1,0:T(8,128)S(1)} %get-tuple-element.123), channel_id=1, source_target_pairs={{4,0},{8,4},{12,8},{16,12},{20,16},{24,20},{28,24},{5,1},{9,5},{13... | collective-permute-start | bytes 92168 | tf_op jit(solution)/shard_map/ppermute | solution.py:48
  109.1 6.3 %collective-permute-start.3 = (f32[3,5,512]{2,1,0:T(8,128)S(1)}, f32[3,5,512]{2,1,0:T(8,128)S(1)}, u32[]{:S(2)}, u32[]{:S(2)}) collective-permute-start(f32[3,5,512]{2,1,0:T(8,128)S(1)} %get-tuple-element.122), channel_id=1, source_target_pairs={{0,4},{4,8},{8,12},{12,16},{16,20},{20,24},{24,28},{1,5},{5,9},{9,... | collective-permute-start | bytes 92168 | tf_op jit(solution)/shard_map/ppermute | solution.py:48
  117.7 1.0 copy-start.4
  117.7 1.3 copy-start.16
  117.7 1.3 copy-start.36
  118.7 0.9 copy-start.22
  119.5 1.2 copy-start.2
  119.5 1.2 copy-start.6
  119.5 1.2 copy-start.8
  119.5 1.2 copy-start.10
  119.5 1.2 copy-start.12
  119.5 1.2 copy-start.14
  120.7 4.2 %copy-start.18 = (f32[3,8,16,16]{3,0,2,1:T(4,128)S(1)}, f32[3,8,16,16]{3,0,2,1:T(4,128)}, u32[]{:S(2)}) copy-start(f32[3,8,16,16]{3,0,2,1:T(4,128)} %copy-done.17) | copy-start | bytes 73732
  134.9 8.7 %copy-start.38 = (f32[16]{0:T(128)S(1)}, f32[16]{0:T(128)}, u32[]{:S(2)}) copy-start(f32[16]{0:T(128)} %copy-done.37) | copy-start | bytes 196
  136.9 14.0 %all-to-all-start.2 = ((f32[8,9,256]{2,1,0:T(8,128)}), f32[8,9,256]{2,1,0:T(8,128)S(1)}, u32[]{:S(2)}, u32[]{:S(2)}) async-start(f32[8,9,256]{2,1,0:T(8,128)} %copy.323), calls=%async_computation.2 | async-start | bytes 262144 | tf_op jit(solution)/shard_map/all_to_all | solution.py:301
  143.6 78.2 %all-gather.4.cloned.1.call-start = ((), (), s32[]{:S(2)}) async-start(), calls=%async_computation.3 | async-start | bytes 2621440 | tf_op jit(solution)/shard_map/all_gather | solution.py:303
  170.4 3.6 %copy-start.28 = (f32[1,2048]{1,0:T(1,128)S(1)}, f32[1,2048]{1,0:T(1,128)}, u32[]{:S(2)}) copy-start(f32[1,2048]{1,0:T(1,128)} %copy-done.27) | copy-start | bytes 24580
  172.3 6.5 %copy-start.20 = (f32[1,2048]{1,0:T(1,128)S(1)}, f32[1,2048]{1,0:T(1,128)}, u32[]{:S(2)}) copy-start(f32[1,2048]{1,0:T(1,128)} %copy-done.19) | copy-start | bytes 24580
  172.3 6.5 %copy-start.33 = (f32[1,2048]{1,0:T(1,128)S(1)}, f32[1,2048]{1,0:T(1,128)}, u32[]{:S(2)}) copy-start(f32[1,2048]{1,0:T(1,128)} %get-tuple-element.81) | copy-start | bytes 24580
  172.3 7.2 %copy-start = (f32[1,2048]{0,1:T(8,128)S(1)}, f32[1,2048]{0,1:T(8,128)}, u32[]{:S(2)}) copy-start(f32[1,2048]{0,1:T(8,128)} %get-tuple-element.99) | copy-start | bytes 24580
  175.5 9.3 %copy-start.32 = (f32[1,2048]{1,0:T(1,128)S(1)}, f32[1,2048]{1,0:T(1,128)}, u32[]{:S(2)}) copy-start(f32[1,2048]{1,0:T(1,128)} %get-tuple-element.91) | copy-start | bytes 24580
  175.5 9.4 %copy-start.31 = (f32[1,2048]{1,0:T(1,128)S(1)}, f32[1,2048]{1,0:T(1,128)}, u32[]{:S(2)}) copy-start(f32[1,2048]{1,0:T(1,128)} %get-tuple-element.93) | copy-start | bytes 24580
  177.1 15.8 %copy-start.29 = (f32[2048]{0:T(1024)S(1)}, f32[2048]{0:T(1024)}, u32[]{:S(2)}) copy-start(f32[2048]{0:T(1024)} %get-tuple-element.165) | copy-start | bytes 24580
  177.1 16.8 %copy-start.26 = (f32[2048]{0:T(1024)S(1)}, f32[2048]{0:T(1024)}, u32[]{:S(2)}) copy-start(f32[2048]{0:T(1024)} %copy-done.25) | copy-start | bytes 24580
  177.1 16.8 %copy-start.24 = (f32[2048]{0:T(1024)S(1)}, f32[2048]{0:T(1024)}, u32[]{:S(2)}) copy-start(f32[2048]{0:T(1024)} %copy-done.23) | copy-start | bytes 24580
  179.5 0.7 copy-start.34
Sparse Core Ops, SparseCore 0:
  201.3 20.3 all-gather.3
